TPU v7x, 32 devices: a whole 2x2x4 slice. The times are simulated.
32 devices in a mesh: img: 8 (over z, y), gy: 4 (over x, core).
Axes of the slice: x: 2, y: 2, z: 4, core: 2. Of those that a mesh axis runs over, the one named last changes fastest.
Arguments:
- path: float32 [32, 4, 128, 128], P('img', None, 'gy'), may hold values from -1.2 to 1.2
- start_image: float32 [4, 128, 128], P(None, 'gy'), may hold values from -1.2 to 1.2
- end_image: float32 [4, 128, 128], P(None, 'gy'), may hold values from -1.2 to 1.2
- labels: int32 [4, 128, 128], P(None, 'gy'), may hold values from 0 to 3
- mob_table: float32 [4], replicated, may hold values from 0.2 to 2
Outputs:
- new_path: float32 [32, 4, 128, 128], P('img', None, 'gy')
All inputs are finite; a program needn't handle non-finite values.
Results may differ from a plain program's by a relative error of at most 0.0001.
Values sent between devices are 32-bit elements; how exact they have to be, the bound alone decides.
No kernel may reach another device: no remote copies, remote signals or barrier semaphores. Data moves between devices by JAX's collectives and lax.ppermute only.
A program may use at most 64 MiB of HBM per device.

v0:
```python
import jax
import jax.numpy as jnp
from jax import lax
from jax.sharding import PartitionSpec as P

ITERS = 2
time_step = 0.5
stiffness = 0.25
step_length = 0.05


def extended_2(shard, sides, width):
    for axis, dim in sides:
        size, length = (lax.axis_size(axis), shard.shape[dim])
        up = [(i, (i + 1) % size) for i in range(size - 1)]
        down = [(j, i) for i, j in up]
        last = lax.slice_in_dim(shard, length - width, length, axis=dim)
        initial = lax.slice_in_dim(shard, 0, width, axis=dim)
        before = lax.ppermute(last, axis, up)
        after = lax.ppermute(initial, axis, down)
        shard = jnp.concatenate([before, shard, after], axis=dim)
    return shard


def shifted(block, axis, distance):
    devices = range(lax.axis_size(axis))
    route = [(i - distance, i) for i in devices if i - distance in devices]
    return lax.ppermute(block, axis, route)


def mobility(labels, table):
    result = jnp.zeros(labels.shape, jnp.float32)
    for level in range(table.shape[0]):
        result = result + jnp.where(labels == level, table[level], jnp.float32(0.0))
    return result


def laplace(padded):
    centre = padded[..., 1:-1, :]
    total = jnp.roll(centre, 1, -3) + jnp.roll(centre, -1, -3)
    total = total + jnp.roll(centre, 1, -1) + jnp.roll(centre, -1, -1)
    return total + padded[..., 2:, :] + padded[..., :-2, :] - 6.0 * centre


def drift(padded, mob):
    centre = padded[..., 1:-1, :]
    return mob * (stiffness * laplace(padded) + centre - centre * centre * centre)


def per_device(path, start_image, end_image, labels, mob_table):
    count = path.shape[0]
    groups = lax.axis_size("img")
    images = count * groups
    rank = lax.axis_index("img")
    is_first = rank == 0
    is_final = rank == groups - 1
    gy_count = lax.axis_size("gy")
    rows_here = path.shape[2]
    cells = images * path.shape[1] * rows_here * gy_count * path.shape[3]
    mob = mobility(labels, mob_table)
    for step in range(ITERS):
        extended = jnp.concatenate([start_image[None], path], 0)
        padded = extended_2(extended, (("gy", 2),), 1)
        force = drift(padded, mob)
        current = padded[1 : count + 1, :, 1:-1, :]
        start_part = padded[0, :, 1:-1, :]
        ahead = shifted(current[0], "img", -1)
        ahead = jnp.where(is_final, end_image, ahead)
        later = jnp.concatenate([current[1:], ahead[None]], 0)
        wide_res = (later - current) / time_step - force[1:]
        opening = (current[0] - start_part) / time_step - force[0]
        mres = mob * wide_res
        mpad = extended_2(mres, (("gy", 2),), 1)
        previous = shifted(wide_res[-1], "img", 1)
        previous = jnp.where(is_first, opening, previous)
        earlier = jnp.concatenate([previous[None], wide_res[:-1]], 0)
        adjoint = stiffness * laplace(mpad) + (1.0 - 3.0 * path * path) * mres
        grad = (earlier - wide_res) / time_step - adjoint
        flat = grad.reshape(count, groups, -1)
        columns = lax.all_to_all(flat, "img", split_axis=1, concat_axis=0, tiled=True)
        every = columns.shape[0]
        index = jnp.arange(1, every + 1).astype(jnp.float32)[:, None, None]
        scaled = index * columns
        before_g = jnp.cumsum(columns, 0) - columns
        before_q = jnp.cumsum(scaled, 0) - scaled
        coeff = jnp.sum(columns, 0) - jnp.sum(scaled, 0) / (every + 1)
        solved = time_step * time_step * (index * coeff[None] - index * before_g + before_q)
        back = lax.all_to_all(solved, "img", split_axis=0, concat_axis=1, tiled=True)
        update = back.reshape(grad.shape)
        squares = lax.psum(jnp.sum(update * update), ("img", "gy"))
        scale = step_length * lax.rsqrt(squares / cells + 1e-06)
        path = path - scale * update
    return path


def solution(mesh):
    in_specs = (
        P("img", None, "gy", None),
        P(None, "gy", None),
        P(None, "gy", None),
        P(None, "gy", None),
        P(),
    )
    out_specs = P("img", None, "gy", None)
    return jax.shard_map(
        per_device, mesh=mesh, in_specs=in_specs, out_specs=out_specs, check_vma=False
    )
```

profile of v0, /device:TPU:0, one launch (start us, length us, event | category | flops | bytes accessed | tf_op | source)
XLA Modules:
  0.0 188.7 jit_solution(131051156970023099)
XLA Ops:
  0.0 0.9 fusion.70
  0.9 1.3 collective-permute-start
  2.2 0.0 copy-start.4
  2.3 3.2 %collective-permute-start.1 = (f32[5,4,1,128]{3,2,1,0:T(1,128)S(1)}, f32[5,4,1,128]{3,2,1,0:T(1,128)S(1)}, u32[]{:S(2)}, u32[]{:S(2)}) collective-permute-start(f32[5,4,1,128]{3,2,1,0:T(1,128)S(1)} %get-tuple-element.32), channel_id=1, source_target_pairs={{0,1},{1,2},{2,3},{4,5},{5,6},{6,7},{8,9},{9,10},{10,11},{12,13},{... | collective-permute-start | bytes 30728 | tf_op jit(solution)/shard_map/ppermute | solution.py:19
  5.4 1.3 collective-permute-start.2
  6.8 0.2 fusion.24
  6.9 0.2 fusion.25
  7.1 0.0 copy-start.6
  7.2 0.6 copy-done.7
  7.7 0.6 fusion.84
  8.4 2.5 %select_add_fusion = f32[4,32,128]{2,1,0:T(8,128)S(1)} fusion(s32[4,32,128]{2,1,0:T(8,128)S(1)} %copy-done.6, f32[]{:T(128)} %bitcast.4, f32[]{:T(128)} %bitcast.3, f32[]{:T(128)} %bitcast.2, f32[]{:T(128)} %bitcast.1), kind=kLoop, calls=%fused_computation.139 | loop fusion | flops 180224 | bytes 131088 | tf_op jit(solution)/shard_map/add | solution.py:34
  10.9 0.0 copy-start.5
  10.9 0.4 fusion.7
  11.3 0.0 slice-start.1
  11.4 1.3 collective-permute-done.2
  12.7 0.1 broadcast_multiply_fusion.3
  12.8 0.1 fusion.79
  12.9 0.1 fusion.80
  13.1 5.3 %collective-permute-start.3 = (f32[4,32,128]{2,1,0:T(8,128)S(1)}, f32[4,32,128]{2,1,0:T(8,128)S(1)}, u32[]{:S(2)}, u32[]{:S(2)}) collective-permute-start(f32[4,32,128]{2,1,0:T(8,128)S(1)} %slice_bitcast_fusion.3), channel_id=1, source_target_pairs={{0,4},{4,8},{8,12},{12,16},{16,20},{20,24},{24,28},{1,5},{5,9},{9,... | collective-permute-start | bytes 196616 | tf_op jit(solution)/shard_map/ppermute | solution.py:28
  18.5 1.3 collective-permute-start.4
  19.8 3.4 %collective-permute-start.5 = (f32[4,4,1,128]{3,2,1,0:T(1,128)S(1)}, f32[4,4,1,128]{3,2,1,0:T(1,128)S(1)}, u32[]{:S(2)}, u32[]{:S(2)}) collective-permute-start(f32[4,4,1,128]{3,2,1,0:T(1,128)S(1)} %get-tuple-element.52), channel_id=1, source_target_pairs={{0,1},{1,2},{2,3},{4,5},{5,6},{6,7},{8,9},{9,10},{10,11},{12,13},{... | collective-permute-start | bytes 24584 | tf_op jit(solution)/shard_map/ppermute | solution.py:19
  23.3 0.8 collective-permute-done.5
  24.0 0.4 fusion.33
  24.5 0.9 copy.6
  25.4 5.7 %all-to-all-start = ((f32[4,8,2048]{2,0,1:T(4,128)}), f32[4,8,2048]{2,0,1:T(4,128)S(1)}, u32[]{:S(2)}, u32[]{:S(2)}) async-start(f32[4,8,2048]{2,0,1:T(4,128)} %copy.6), calls=%async_computation | async-start | bytes 524288 | tf_op jit(solution)/shard_map/all_to_all | solution.py:80
  31.1 9.8 %all-to-all-done = f32[4,8,2048]{2,0,1:T(4,128)S(1)} async-done(((f32[4,8,2048]{2,0,1:T(4,128)}), f32[4,8,2048]{2,0,1:T(4,128)S(1)}, u32[]{:S(2)}, u32[]{:S(2)}) %all-to-all-start) | async-done | bytes 262176 | tf_op jit(solution)/shard_map/all_to_all | solution.py:80
  40.9 0.2 all_to_all.41
  41.1 0.3 fusion.73
  41.4 0.2 fusion.85
  41.6 0.1 reduce_sum.54
  41.7 0.7 add_multiply_fusion.1
  42.4 13.0 %all_to_all.54 = f32[32,1,2048]{2,1,0:T(1,128)S(1)} all-to-all(f32[32,1,2048]{2,1,0:T(1,128)S(1)} %add_multiply_fusion.1), channel_id=1, replica_groups=mesh['img'=8,'gy'=4] {'img'}, dimensions={0} | all-to-all | bytes 524288 | tf_op jit(solution)/shard_map/all_to_all | solution.py:88
  55.4 1.1 multiply_reduce_fusion.1
  56.6 38.9 %psum.14 = f32[]{:T(128)} all-reduce(f32[]{:T(128)} %multiply_reduce_fusion.1), channel_id=1, replica_groups=mesh['img'=8,'gy'=4] {'img','gy'}, use_global_device_ids=true, to_apply=%region_5.6 | all-reduce | flops 1 | bytes 8 | tf_op jit(solution)/shard_map/psum | solution.py:90
  96.2 0.2 copy.7
  96.5 0.2 fusion.20
  96.6 0.2 fusion.21
  96.9 1.3 collective-permute-start.6
  98.2 3.0 %collective-permute-start.7 = (f32[5,4,1,128]{3,2,1,0:T(1,128)S(1)}, f32[5,4,1,128]{3,2,1,0:T(1,128)S(1)}, u32[]{:S(2)}, u32[]{:S(2)}) collective-permute-start(f32[5,4,1,128]{3,2,1,0:T(1,128)S(1)} %get-tuple-element.22), channel_id=1, source_target_pairs={{0,1},{1,2},{2,3},{4,5},{5,6},{6,7},{8,9},{9,10},{10,11},{12,13},{... | collective-permute-start | bytes 30728 | tf_op jit(solution)/shard_map/ppermute | solution.py:19
  101.2 1.3 collective-permute-start.8
  102.6 0.4 fusion.15
  103.0 0.0 slice-start
  103.0 5.1 %collective-permute-done.8 = f32[4,32,128]{2,1,0:T(8,128)S(1)} collective-permute-done((f32[4,32,128]{2,1,0:T(8,128)S(1)}, f32[4,32,128]{2,1,0:T(8,128)S(1)}, u32[]{:S(2)}, u32[]{:S(2)}) %collective-permute-start.8) | collective-permute-done | bytes 65568 | tf_op jit(solution)/shard_map/ppermute | solution.py:28
  108.1 1.0 broadcast_multiply_fusion.2
  109.1 0.1 fusion.74
  109.3 0.1 fusion.75
  109.5 0.0 copy-start.1
  109.5 4.7 %collective-permute-start.9 = (f32[4,32,128]{2,1,0:T(8,128)S(1)}, f32[4,32,128]{2,1,0:T(8,128)S(1)}, u32[]{:S(2)}, u32[]{:S(2)}) collective-permute-start(f32[4,32,128]{2,1,0:T(8,128)S(1)} %slice_bitcast_fusion), channel_id=1, source_target_pairs={{0,4},{4,8},{8,12},{12,16},{16,20},{20,24},{24,28},{1,5},{5,9},{9,... | collective-permute-start | bytes 196616 | tf_op jit(solution)/shard_map/ppermute | solution.py:28
  114.3 1.3 collective-permute-start.10
  115.6 3.0 %collective-permute-start.11 = (f32[4,4,1,128]{3,2,1,0:T(1,128)S(1)}, f32[4,4,1,128]{3,2,1,0:T(1,128)S(1)}, u32[]{:S(2)}, u32[]{:S(2)}) collective-permute-start(f32[4,4,1,128]{3,2,1,0:T(1,128)S(1)} %get-tuple-element.42), channel_id=1, source_target_pairs={{0,1},{1,2},{2,3},{4,5},{5,6},{6,7},{8,9},{9,10},{10,11},{12,13},{... | collective-permute-start | bytes 24584 | tf_op jit(solution)/shard_map/ppermute | solution.py:19
  118.7 0.8 collective-permute-done.11
  119.4 0.4 fusion.37
  119.9 0.2 copy.8
  120.1 12.8 %all_to_all.55 = f32[4,8,2048]{2,0,1:T(4,128)S(1)} all-to-all(f32[4,8,2048]{2,0,1:T(4,128)S(1)} %copy.8), channel_id=1, replica_groups=mesh['img'=8,'gy'=4] {'img'}, dimensions={1} | all-to-all | bytes 524288 | tf_op jit(solution)/shard_map/all_to_all | solution.py:80
  132.9 0.2 all_to_all.46
  133.1 0.3 fusion.72
  133.4 0.2 fusion.86
  133.6 0.1 reduce_sum.57
  133.6 0.7 add_multiply_fusion
  134.3 12.6 %all_to_all.56 = f32[32,1,2048]{2,1,0:T(1,128)S(1)} all-to-all(f32[32,1,2048]{2,1,0:T(1,128)S(1)} %add_multiply_fusion), channel_id=1, replica_groups=mesh['img'=8,'gy'=4] {'img'}, dimensions={0} | all-to-all | bytes 524288 | tf_op jit(solution)/shard_map/all_to_all | solution.py:88
  147.0 1.1 multiply_reduce_fusion
  148.1 38.9 %psum.15 = f32[]{:T(128)} all-reduce(f32[]{:T(128)} %multiply_reduce_fusion), channel_id=1, replica_groups=mesh['img'=8,'gy'=4] {'img','gy'}, use_global_device_ids=true, to_apply=%region_11.12 | all-reduce | flops 1 | bytes 8 | tf_op jit(solution)/shard_map/psum | solution.py:90
  187.7 0.2 copy.9
  187.9 0.7 sub.179
  (52 shorter events, 0.7 us)
Async XLA Ops:
  0.0 5.4 %copy-start.2 = (f32[4,4,32,128]{3,2,1,0:T(8,128)S(1)}, f32[4,4,32,128]{3,2,1,0:T(8,128)}, u32[]{:S(2)}) copy-start(f32[4,4,32,128]{3,2,1,0:T(8,128)} %param.5) | copy-start | bytes 786436
  0.9 10.0 %collective-permute-start = (f32[5,4,1,128]{3,2,1,0:T(1,128)S(1)}, f32[5,4,1,128]{3,2,1,0:T(1,128)S(1)}, u32[]{:S(2)}, u32[]{:S(2)}) collective-permute-start(f32[5,4,1,128]{3,2,1,0:T(1,128)S(1)} %get-tuple-element.31), channel_id=1, source_target_pairs={{1,0},{2,1},{3,2},{5,4},{6,5},{7,6},{9,8},{10,9},{11,10},{13,12},{... | collective-permute-start | bytes 30728 | tf_op jit(solution)/shard_map/ppermute | solution.py:20
  2.2 4.5 %copy-start.4 = (f32[4,32,128]{2,1,0:T(8,128)S(1)}, f32[4,32,128]{2,1,0:T(8,128)}, u32[]{:S(2)}) copy-start(f32[4,32,128]{2,1,0:T(8,128)} %param.6) | copy-start | bytes 196612
  2.3 8.7 %collective-permute-start.1 = (f32[5,4,1,128]{3,2,1,0:T(1,128)S(1)}, f32[5,4,1,128]{3,2,1,0:T(1,128)S(1)}, u32[]{:S(2)}, u32[]{:S(2)}) collective-permute-start(f32[5,4,1,128]{3,2,1,0:T(1,128)S(1)} %get-tuple-element.32), channel_id=1, source_target_pairs={{0,1},{1,2},{2,3},{4,5},{5,6},{6,7},{8,9},{9,10},{10,11},{12,13},{... | collective-permute-start | bytes 30728 | tf_op jit(solution)/shard_map/ppermute | solution.py:19
  5.4 7.2 %collective-permute-start.2 = (f32[4,32,128]{2,1,0:T(8,128)S(1)}, f32[4,32,128]{2,1,0:T(8,128)S(1)}, u32[]{:S(2)}, u32[]{:S(2)}) collective-permute-start(f32[4,32,128]{2,1,0:T(8,128)S(1)} %slice_bitcast_fusion.5), channel_id=1, source_target_pairs={{4,0},{8,4},{12,8},{16,12},{20,16},{24,20},{28,24},{5,1},{9,5},{13... | collective-permute-start | bytes 196616 | tf_op jit(solution)/shard_map/ppermute | solution.py:28
  7.1 0.7 copy-start.7
  7.1 1.3 copy-start.6
  10.9 1.7 copy-start.5
  10.9 1.7 copy-start.3
  11.3 1.3 slice-start.1
  13.1 10.1 %collective-permute-start.3 = (f32[4,32,128]{2,1,0:T(8,128)S(1)}, f32[4,32,128]{2,1,0:T(8,128)S(1)}, u32[]{:S(2)}, u32[]{:S(2)}) collective-permute-start(f32[4,32,128]{2,1,0:T(8,128)S(1)} %slice_bitcast_fusion.3), channel_id=1, source_target_pairs={{0,4},{4,8},{8,12},{12,16},{16,20},{20,24},{24,28},{1,5},{5,9},{9,... | collective-permute-start | bytes 196616 | tf_op jit(solution)/shard_map/ppermute | solution.py:28
  18.5 4.8 %collective-permute-start.4 = (f32[4,4,1,128]{3,2,1,0:T(1,128)S(1)}, f32[4,4,1,128]{3,2,1,0:T(1,128)S(1)}, u32[]{:S(2)}, u32[]{:S(2)}) collective-permute-start(f32[4,4,1,128]{3,2,1,0:T(1,128)S(1)} %get-tuple-element.51), channel_id=1, source_target_pairs={{1,0},{2,1},{3,2},{5,4},{6,5},{7,6},{9,8},{10,9},{11,10},{13,12},{... | collective-permute-start | bytes 24584 | tf_op jit(solution)/shard_map/ppermute | solution.py:20
  19.8 4.2 %collective-permute-start.5 = (f32[4,4,1,128]{3,2,1,0:T(1,128)S(1)}, f32[4,4,1,128]{3,2,1,0:T(1,128)S(1)}, u32[]{:S(2)}, u32[]{:S(2)}) collective-permute-start(f32[4,4,1,128]{3,2,1,0:T(1,128)S(1)} %get-tuple-element.52), channel_id=1, source_target_pairs={{0,1},{1,2},{2,3},{4,5},{5,6},{6,7},{8,9},{9,10},{10,11},{12,13},{... | collective-permute-start | bytes 24584 | tf_op jit(solution)/shard_map/ppermute | solution.py:19
  25.4 15.6 %all-to-all-start = ((f32[4,8,2048]{2,0,1:T(4,128)}), f32[4,8,2048]{2,0,1:T(4,128)S(1)}, u32[]{:S(2)}, u32[]{:S(2)}) async-start(f32[4,8,2048]{2,0,1:T(4,128)} %copy.6), calls=%async_computation | async-start | bytes 524288 | tf_op jit(solution)/shard_map/all_to_all | solution.py:80
  96.5 6.1 %copy-start = (f32[4,4,32,128]{3,2,1,0:T(8,128)}, f32[4,4,32,128]{3,2,1,0:T(8,128)S(1)}, u32[]{:S(2)}) copy-start(f32[4,4,32,128]{3,2,1,0:T(8,128)S(1)} %sub.164) | copy-start | bytes 786436
  96.9 5.7 %collective-permute-start.6 = (f32[5,4,1,128]{3,2,1,0:T(1,128)S(1)}, f32[5,4,1,128]{3,2,1,0:T(1,128)S(1)}, u32[]{:S(2)}, u32[]{:S(2)}) collective-permute-start(f32[5,4,1,128]{3,2,1,0:T(1,128)S(1)} %get-tuple-element.21), channel_id=1, source_target_pairs={{1,0},{2,1},{3,2},{5,4},{6,5},{7,6},{9,8},{10,9},{11,10},{13,12},{... | collective-permute-start | bytes 30728 | tf_op jit(solution)/shard_map/ppermute | solution.py:20
  98.2 4.4 %collective-permute-start.7 = (f32[5,4,1,128]{3,2,1,0:T(1,128)S(1)}, f32[5,4,1,128]{3,2,1,0:T(1,128)S(1)}, u32[]{:S(2)}, u32[]{:S(2)}) collective-permute-start(f32[5,4,1,128]{3,2,1,0:T(1,128)S(1)} %get-tuple-element.22), channel_id=1, source_target_pairs={{0,1},{1,2},{2,3},{4,5},{5,6},{6,7},{8,9},{9,10},{10,11},{12,13},{... | collective-permute-start | bytes 30728 | tf_op jit(solution)/shard_map/ppermute | solution.py:19
  101.2 6.8 %collective-permute-start.8 = (f32[4,32,128]{2,1,0:T(8,128)S(1)}, f32[4,32,128]{2,1,0:T(8,128)S(1)}, u32[]{:S(2)}, u32[]{:S(2)}) collective-permute-start(f32[4,32,128]{2,1,0:T(8,128)S(1)} %slice_bitcast_fusion.2), channel_id=1, source_target_pairs={{4,0},{8,4},{12,8},{16,12},{20,16},{24,20},{28,24},{5,1},{9,5},{13... | collective-permute-start | bytes 196616 | tf_op jit(solution)/shard_map/ppermute | solution.py:28
  103.0 5.1 %slice-start = ((f32[4,4,32,128]{3,2,1,0:T(8,128)}), f32[3,4,32,128]{3,2,1,0:T(8,128)S(1)}, s32[]{:S(2)}) async-start(f32[4,4,32,128]{3,2,1,0:T(8,128)} %copy-done), calls=%async_computation.4 | async-start | bytes 393216 | tf_op jit(solution)/shard_map/slice | solution.py:69
  109.5 9.2 %copy-start.1 = (f32[4,4,32,128]{3,2,1,0:T(8,128)S(1)}, f32[4,4,32,128]{3,2,1,0:T(8,128)}, u32[]{:S(2)}) copy-start(f32[4,4,32,128]{3,2,1,0:T(8,128)} %copy-done) | copy-start | bytes 786436
  109.5 9.1 %collective-permute-start.9 = (f32[4,32,128]{2,1,0:T(8,128)S(1)}, f32[4,32,128]{2,1,0:T(8,128)S(1)}, u32[]{:S(2)}, u32[]{:S(2)}) collective-permute-start(f32[4,32,128]{2,1,0:T(8,128)S(1)} %slice_bitcast_fusion), channel_id=1, source_target_pairs={{0,4},{4,8},{8,12},{12,16},{16,20},{20,24},{24,28},{1,5},{5,9},{9,... | collective-permute-start | bytes 196616 | tf_op jit(solution)/shard_map/ppermute | solution.py:28
  114.3 4.4 %collective-permute-start.10 = (f32[4,4,1,128]{3,2,1,0:T(1,128)S(1)}, f32[4,4,1,128]{3,2,1,0:T(1,128)S(1)}, u32[]{:S(2)}, u32[]{:S(2)}) collective-permute-start(f32[4,4,1,128]{3,2,1,0:T(1,128)S(1)} %get-tuple-element.41), channel_id=1, source_target_pairs={{1,0},{2,1},{3,2},{5,4},{6,5},{7,6},{9,8},{10,9},{11,10},{13,12},{... | collective-permute-start | bytes 24584 | tf_op jit(solution)/shard_map/ppermute | solution.py:20
  115.6 3.8 %collective-permute-start.11 = (f32[4,4,1,128]{3,2,1,0:T(1,128)S(1)}, f32[4,4,1,128]{3,2,1,0:T(1,128)S(1)}, u32[]{:S(2)}, u32[]{:S(2)}) collective-permute-start(f32[4,4,1,128]{3,2,1,0:T(1,128)S(1)} %get-tuple-element.42), channel_id=1, source_target_pairs={{0,1},{1,2},{2,3},{4,5},{5,6},{6,7},{8,9},{9,10},{10,11},{12,13},{... | collective-permute-start | bytes 24584 | tf_op jit(solution)/shard_map/ppermute | solution.py:19
where the time goes:
time: 190 us; the launch traced here: 189 us
  blocking collectives  116 us (61%)
  starting transfers between devices  36.1 us (19%)
  waiting for transfers between devices  17.7 us (9%)
  other arithmetic  12.6 us (7%)
  local copies, waits for them, and re-layouts  3.91 us (2%)
  between operations  2.03 us (1%)
    psum x2, blocking collectives, per_device(): squares = lax.psum(jnp.sum(update * update), ('img', 'gy'))  77.8 us
    all_to_all x2, blocking collectives, per_device(): lax.all_to_all(solved, 'img', split_axis=0, concat_axis=1, tiled=True)  25.7 us
    all_to_all x1, blocking collectives, per_device(): lax.all_to_all(flat, 'img', split_axis=1, concat_axis=0, tiled=True)  12.8 us
    ppermute x4, starting transfers between devices, extended_2(): before = lax.ppermute(last, axis, up)  12.6 us
    ppermute x4, starting transfers between devices, shifted(): return lax.ppermute(block, axis, route)  12.6 us
    all_to_all x1, waiting for transfers between devices, per_device(): lax.all_to_all(flat, 'img', split_axis=1, concat_axis=0, tiled=True)  9.83 us
    ppermute x4, waiting for transfers between devices, shifted(): return lax.ppermute(block, axis, route)  6.37 us
    all_to_all x1, starting transfers between devices, per_device(): lax.all_to_all(flat, 'img', split_axis=1, concat_axis=0, tiled=True)  5.72 us
  transfers between devices with their start and end apart: 13, of which 5 were waited for; matrix products, arithmetic and copies ran while one was open for 2% of the time, Pallas kernels for 0%

commit v1 on v0

--- a/solution.py
+++ b/solution.py
@@ -85,7 +85,10 @@
         before_q = jnp.cumsum(scaled, 0) - scaled
         coeff = jnp.sum(columns, 0) - jnp.sum(scaled, 0) / (every + 1)
         solved = time_step * time_step * (index * coeff[None] - index * before_g + before_q)
-        back = lax.all_to_all(solved, "img", split_axis=0, concat_axis=1, tiled=True)
+        back = jnp.concatenate(
+            lax.all_to_all(jnp.stack(jnp.split(solved, lax.axis_size("img"), axis=0)), "img", 0, 0),
+            axis=1,
+        )
         update = back.reshape(grad.shape)
         squares = lax.psum(jnp.sum(update * update), ("img", "gy"))
         scale = step_length * lax.rsqrt(squares / cells + 1e-06)

time: 190 us -> 190 us (level)
  no operation moved by 1% of the time
where the time goes in v1:
time: 190 us; the launch traced here: 189 us
  blocking collectives  116 us (61%)
  starting transfers between devices  36.1 us (19%)
  waiting for transfers between devices  17.7 us (9%)
  other arithmetic  12.9 us (7%)
  local copies, waits for them, and re-layouts  4.07 us (2%)
  between operations  2.11 us (1%)
    psum x2, blocking collectives, per_device(): squares = lax.psum(jnp.sum(update * update), ('img', 'gy'))  77.8 us
    all_to_all x2, blocking collectives, per_device(): lax.all_to_all(jnp.stack(jnp.split(solved, lax.axis_size('img'), axis=0))...  25.7 us
    all_to_all x1, blocking collectives, per_device(): lax.all_to_all(flat, 'img', split_axis=1, concat_axis=0, tiled=True)  12.8 us
    ppermute x4, starting transfers between devices, extended_2(): before = lax.ppermute(last, axis, up)  12.6 us
    ppermute x4, starting transfers between devices, shifted(): return lax.ppermute(block, axis, route)  12.6 us
    all_to_all x1, waiting for transfers between devices, per_device(): lax.all_to_all(flat, 'img', split_axis=1, concat_axis=0, tiled=True)  9.83 us
    ppermute x4, waiting for transfers between devices, shifted(): return lax.ppermute(block, axis, route)  6.37 us
    all_to_all x1, starting transfers between devices, per_device(): lax.all_to_all(flat, 'img', split_axis=1, concat_axis=0, tiled=True)  5.72 us
  transfers between devices with their start and end apart: 13, of which 5 were waited for; matrix products, arithmetic and copies ran while one was open for 2% of the time, Pallas kernels for 0%

profile of v1, /device:TPU:0, one launch (start us, length us, event | category | flops | bytes accessed | tf_op | source)
XLA Modules:
  0.0 189.3 jit_solution(7907299605925975271)
XLA Ops:
  0.0 0.9 fusion.70
  0.9 1.3 collective-permute-start
  2.2 0.0 copy-start.4
  2.3 3.2 %collective-permute-start.1 = (f32[5,4,1,128]{3,2,1,0:T(1,128)S(1)}, f32[5,4,1,128]{3,2,1,0:T(1,128)S(1)}, u32[]{:S(2)}, u32[]{:S(2)}) collective-permute-start(f32[5,4,1,128]{3,2,1,0:T(1,128)S(1)} %get-tuple-element.32), channel_id=1, source_target_pairs={{0,1},{1,2},{2,3},{4,5},{5,6},{6,7},{8,9},{9,10},{10,11},{12,13},{... | collective-permute-start | bytes 30728 | tf_op jit(solution)/shard_map/ppermute | solution.py:19
  5.4 1.3 collective-permute-start.2
  6.8 0.2 fusion.24
  6.9 0.2 fusion.25
  7.2 0.6 copy-done.7
  7.7 0.6 fusion.84
  8.4 2.5 %select_add_fusion = f32[4,32,128]{2,1,0:T(8,128)S(1)} fusion(s32[4,32,128]{2,1,0:T(8,128)S(1)} %copy-done.6, f32[]{:T(128)} %bitcast.4, f32[]{:T(128)} %bitcast.3, f32[]{:T(128)} %bitcast.2, f32[]{:T(128)} %bitcast.1), kind=kLoop, calls=%fused_computation.139 | loop fusion | flops 180224 | bytes 131088 | tf_op jit(solution)/shard_map/add | solution.py:34
  10.9 0.0 copy-start.5
  10.9 0.4 fusion.7
  11.3 0.0 slice-start.1
  11.4 1.3 collective-permute-done.2
  12.7 0.1 broadcast_multiply_fusion.1
  12.8 0.1 fusion.79
  12.9 0.1 fusion.80
  13.1 5.3 %collective-permute-start.3 = (f32[4,32,128]{2,1,0:T(8,128)S(1)}, f32[4,32,128]{2,1,0:T(8,128)S(1)}, u32[]{:S(2)}, u32[]{:S(2)}) collective-permute-start(f32[4,32,128]{2,1,0:T(8,128)S(1)} %slice_bitcast_fusion.3), channel_id=1, source_target_pairs={{0,4},{4,8},{8,12},{12,16},{16,20},{20,24},{24,28},{1,5},{5,9},{9,... | collective-permute-start | bytes 196616 | tf_op jit(solution)/shard_map/ppermute | solution.py:28
  18.5 1.3 collective-permute-start.4
  19.8 3.4 %collective-permute-start.5 = (f32[4,4,1,128]{3,2,1,0:T(1,128)S(1)}, f32[4,4,1,128]{3,2,1,0:T(1,128)S(1)}, u32[]{:S(2)}, u32[]{:S(2)}) collective-permute-start(f32[4,4,1,128]{3,2,1,0:T(1,128)S(1)} %get-tuple-element.52), channel_id=1, source_target_pairs={{0,1},{1,2},{2,3},{4,5},{5,6},{6,7},{8,9},{9,10},{10,11},{12,13},{... | collective-permute-start | bytes 24584 | tf_op jit(solution)/shard_map/ppermute | solution.py:19
  23.3 0.8 collective-permute-done.5
  24.0 0.4 fusion.33
  24.5 0.9 copy.8
  25.4 5.7 %all-to-all-start = ((f32[4,8,2048]{2,0,1:T(4,128)}), f32[4,8,2048]{2,0,1:T(4,128)S(1)}, u32[]{:S(2)}, u32[]{:S(2)}) async-start(f32[4,8,2048]{2,0,1:T(4,128)} %copy.8), calls=%async_computation | async-start | bytes 524288 | tf_op jit(solution)/shard_map/all_to_all | solution.py:80
  31.1 9.8 %all-to-all-done = f32[4,8,2048]{2,0,1:T(4,128)S(1)} async-done(((f32[4,8,2048]{2,0,1:T(4,128)}), f32[4,8,2048]{2,0,1:T(4,128)S(1)}, u32[]{:S(2)}, u32[]{:S(2)}) %all-to-all-start) | async-done | bytes 262176 | tf_op jit(solution)/shard_map/all_to_all | solution.py:80
  40.9 0.2 all_to_all.33
  41.1 0.3 fusion.73
  41.4 0.2 fusion.85
  41.6 0.1 reduce_sum.54
  41.7 0.7 add_multiply_fusion.1
  42.5 13.0 %all_to_all.46 = f32[8,4,1,2048]{3,2,1,0:T(1,128)S(1)} all-to-all(f32[8,4,1,2048]{3,2,1,0:T(1,128)S(1)} %constant_dynamic-update-slice_fusion), channel_id=1, replica_groups=mesh['img'=8,'gy'=4] {'img'}, dimensions={0} | all-to-all | bytes 524288 | tf_op jit(solution)/shard_map/all_to_all | solution.py:89
  55.5 1.1 multiply_reduce_fusion.1
  56.7 38.9 %psum.14 = f32[]{:T(128)} all-reduce(f32[]{:T(128)} %multiply_reduce_fusion.1), channel_id=1, replica_groups=mesh['img'=8,'gy'=4] {'img','gy'}, use_global_device_ids=true, to_apply=%region_5.6 | all-reduce | flops 1 | bytes 8 | tf_op jit(solution)/shard_map/psum | solution.py:93
  96.3 0.2 multiply_bitcast_fusion.1
  96.5 0.2 copy.9
  96.7 0.2 fusion.20
  96.9 0.2 fusion.21
  97.2 1.3 collective-permute-start.6
  98.5 3.0 %collective-permute-start.7 = (f32[5,4,1,128]{3,2,1,0:T(1,128)S(1)}, f32[5,4,1,128]{3,2,1,0:T(1,128)S(1)}, u32[]{:S(2)}, u32[]{:S(2)}) collective-permute-start(f32[5,4,1,128]{3,2,1,0:T(1,128)S(1)} %get-tuple-element.22), channel_id=1, source_target_pairs={{0,1},{1,2},{2,3},{4,5},{5,6},{6,7},{8,9},{9,10},{10,11},{12,13},{... | collective-permute-start | bytes 30728 | tf_op jit(solution)/shard_map/ppermute | solution.py:19
  101.5 1.3 collective-permute-start.8
  102.9 0.4 fusion.15
  103.3 0.0 slice-start
  103.3 5.1 %collective-permute-done.8 = f32[4,32,128]{2,1,0:T(8,128)S(1)} collective-permute-done((f32[4,32,128]{2,1,0:T(8,128)S(1)}, f32[4,32,128]{2,1,0:T(8,128)S(1)}, u32[]{:S(2)}, u32[]{:S(2)}) %collective-permute-start.8) | collective-permute-done | bytes 65568 | tf_op jit(solution)/shard_map/ppermute | solution.py:28
  108.4 1.0 broadcast_multiply_fusion
  109.4 0.1 fusion.74
  109.6 0.1 fusion.75
  109.8 4.7 %collective-permute-start.9 = (f32[4,32,128]{2,1,0:T(8,128)S(1)}, f32[4,32,128]{2,1,0:T(8,128)S(1)}, u32[]{:S(2)}, u32[]{:S(2)}) collective-permute-start(f32[4,32,128]{2,1,0:T(8,128)S(1)} %slice_bitcast_fusion), channel_id=1, source_target_pairs={{0,4},{4,8},{8,12},{12,16},{16,20},{20,24},{24,28},{1,5},{5,9},{9,... | collective-permute-start | bytes 196616 | tf_op jit(solution)/shard_map/ppermute | solution.py:28
  114.6 1.3 collective-permute-start.10
  115.9 3.0 %collective-permute-start.11 = (f32[4,4,1,128]{3,2,1,0:T(1,128)S(1)}, f32[4,4,1,128]{3,2,1,0:T(1,128)S(1)}, u32[]{:S(2)}, u32[]{:S(2)}) collective-permute-start(f32[4,4,1,128]{3,2,1,0:T(1,128)S(1)} %get-tuple-element.42), channel_id=1, source_target_pairs={{0,1},{1,2},{2,3},{4,5},{5,6},{6,7},{8,9},{9,10},{10,11},{12,13},{... | collective-permute-start | bytes 24584 | tf_op jit(solution)/shard_map/ppermute | solution.py:19
  119.0 0.8 collective-permute-done.11
  119.7 0.4 fusion.37
  120.2 0.2 copy.10
  120.3 12.8 %all_to_all.47 = f32[4,8,2048]{2,0,1:T(4,128)S(1)} all-to-all(f32[4,8,2048]{2,0,1:T(4,128)S(1)} %copy.10), channel_id=1, replica_groups=mesh['img'=8,'gy'=4] {'img'}, dimensions={1} | all-to-all | bytes 524288 | tf_op jit(solution)/shard_map/all_to_all | solution.py:80
  133.2 0.2 all_to_all.38
  133.3 0.3 fusion.72
  133.7 0.2 fusion.86
  133.9 0.1 reduce_sum.57
  133.9 0.7 add_multiply_fusion
  134.7 12.6 %all_to_all.48 = f32[8,4,1,2048]{3,2,1,0:T(1,128)S(1)} all-to-all(f32[8,4,1,2048]{3,2,1,0:T(1,128)S(1)} %constant_dynamic-update-slice_fusion.8), channel_id=1, replica_groups=mesh['img'=8,'gy'=4] {'img'}, dimensions={0} | all-to-all | bytes 524288 | tf_op jit(solution)/shard_map/all_to_all | solution.py:89
  147.4 1.1 multiply_reduce_fusion
  148.5 38.9 %psum.15 = f32[]{:T(128)} all-reduce(f32[]{:T(128)} %multiply_reduce_fusion), channel_id=1, replica_groups=mesh['img'=8,'gy'=4] {'img','gy'}, use_global_device_ids=true, to_apply=%region_11.12 | all-reduce | flops 1 | bytes 8 | tf_op jit(solution)/shard_map/psum | solution.py:93
  188.1 0.2 multiply_bitcast_fusion
  188.3 0.2 copy.11
  188.5 0.7 sub.179
  (68 shorter events, 0.8 us)
Async XLA Ops:
  0.0 5.4 %copy-start.2 = (f32[4,4,32,128]{3,2,1,0:T(8,128)S(1)}, f32[4,4,32,128]{3,2,1,0:T(8,128)}, u32[]{:S(2)}) copy-start(f32[4,4,32,128]{3,2,1,0:T(8,128)} %param.5) | copy-start | bytes 786436
  0.9 10.0 %collective-permute-start = (f32[5,4,1,128]{3,2,1,0:T(1,128)S(1)}, f32[5,4,1,128]{3,2,1,0:T(1,128)S(1)}, u32[]{:S(2)}, u32[]{:S(2)}) collective-permute-start(f32[5,4,1,128]{3,2,1,0:T(1,128)S(1)} %get-tuple-element.31), channel_id=1, source_target_pairs={{1,0},{2,1},{3,2},{5,4},{6,5},{7,6},{9,8},{10,9},{11,10},{13,12},{... | collective-permute-start | bytes 30728 | tf_op jit(solution)/shard_map/ppermute | solution.py:20
  2.2 4.5 %copy-start.4 = (f32[4,32,128]{2,1,0:T(8,128)S(1)}, f32[4,32,128]{2,1,0:T(8,128)}, u32[]{:S(2)}) copy-start(f32[4,32,128]{2,1,0:T(8,128)} %param.6) | copy-start | bytes 196612
  2.3 8.7 %collective-permute-start.1 = (f32[5,4,1,128]{3,2,1,0:T(1,128)S(1)}, f32[5,4,1,128]{3,2,1,0:T(1,128)S(1)}, u32[]{:S(2)}, u32[]{:S(2)}) collective-permute-start(f32[5,4,1,128]{3,2,1,0:T(1,128)S(1)} %get-tuple-element.32), channel_id=1, source_target_pairs={{0,1},{1,2},{2,3},{4,5},{5,6},{6,7},{8,9},{9,10},{10,11},{12,13},{... | collective-permute-start | bytes 30728 | tf_op jit(solution)/shard_map/ppermute | solution.py:19
  5.4 7.2 %collective-permute-start.2 = (f32[4,32,128]{2,1,0:T(8,128)S(1)}, f32[4,32,128]{2,1,0:T(8,128)S(1)}, u32[]{:S(2)}, u32[]{:S(2)}) collective-permute-start(f32[4,32,128]{2,1,0:T(8,128)S(1)} %slice_bitcast_fusion.5), channel_id=1, source_target_pairs={{4,0},{8,4},{12,8},{16,12},{20,16},{24,20},{28,24},{5,1},{9,5},{13... | collective-permute-start | bytes 196616 | tf_op jit(solution)/shard_map/ppermute | solution.py:28
  7.1 0.7 copy-start.7
  7.1 1.3 copy-start.6
  10.9 1.7 copy-start.5
  10.9 1.7 copy-start.3
  11.3 1.3 slice-start.1
  13.1 10.1 %collective-permute-start.3 = (f32[4,32,128]{2,1,0:T(8,128)S(1)}, f32[4,32,128]{2,1,0:T(8,128)S(1)}, u32[]{:S(2)}, u32[]{:S(2)}) collective-permute-start(f32[4,32,128]{2,1,0:T(8,128)S(1)} %slice_bitcast_fusion.3), channel_id=1, source_target_pairs={{0,4},{4,8},{8,12},{12,16},{16,20},{20,24},{24,28},{1,5},{5,9},{9,... | collective-permute-start | bytes 196616 | tf_op jit(solution)/shard_map/ppermute | solution.py:28
  18.5 4.8 %collective-permute-start.4 = (f32[4,4,1,128]{3,2,1,0:T(1,128)S(1)}, f32[4,4,1,128]{3,2,1,0:T(1,128)S(1)}, u32[]{:S(2)}, u32[]{:S(2)}) collective-permute-start(f32[4,4,1,128]{3,2,1,0:T(1,128)S(1)} %get-tuple-element.51), channel_id=1, source_target_pairs={{1,0},{2,1},{3,2},{5,4},{6,5},{7,6},{9,8},{10,9},{11,10},{13,12},{... | collective-permute-start | bytes 24584 | tf_op jit(solution)/shard_map/ppermute | solution.py:20
  19.8 4.2 %collective-permute-start.5 = (f32[4,4,1,128]{3,2,1,0:T(1,128)S(1)}, f32[4,4,1,128]{3,2,1,0:T(1,128)S(1)}, u32[]{:S(2)}, u32[]{:S(2)}) collective-permute-start(f32[4,4,1,128]{3,2,1,0:T(1,128)S(1)} %get-tuple-element.52), channel_id=1, source_target_pairs={{0,1},{1,2},{2,3},{4,5},{5,6},{6,7},{8,9},{9,10},{10,11},{12,13},{... | collective-permute-start | bytes 24584 | tf_op jit(solution)/shard_map/ppermute | solution.py:19
  25.4 15.6 %all-to-all-start = ((f32[4,8,2048]{2,0,1:T(4,128)}), f32[4,8,2048]{2,0,1:T(4,128)S(1)}, u32[]{:S(2)}, u32[]{:S(2)}) async-start(f32[4,8,2048]{2,0,1:T(4,128)} %copy.8), calls=%async_computation | async-start | bytes 524288 | tf_op jit(solution)/shard_map/all_to_all | solution.py:80
  96.7 6.1 %copy-start = (f32[4,4,32,128]{3,2,1,0:T(8,128)}, f32[4,4,32,128]{3,2,1,0:T(8,128)S(1)}, u32[]{:S(2)}) copy-start(f32[4,4,32,128]{3,2,1,0:T(8,128)S(1)} %sub.164) | copy-start | bytes 786436
  97.2 5.7 %collective-permute-start.6 = (f32[5,4,1,128]{3,2,1,0:T(1,128)S(1)}, f32[5,4,1,128]{3,2,1,0:T(1,128)S(1)}, u32[]{:S(2)}, u32[]{:S(2)}) collective-permute-start(f32[5,4,1,128]{3,2,1,0:T(1,128)S(1)} %get-tuple-element.21), channel_id=1, source_target_pairs={{1,0},{2,1},{3,2},{5,4},{6,5},{7,6},{9,8},{10,9},{11,10},{13,12},{... | collective-permute-start | bytes 30728 | tf_op jit(solution)/shard_map/ppermute | solution.py:20
  98.5 4.4 %collective-permute-start.7 = (f32[5,4,1,128]{3,2,1,0:T(1,128)S(1)}, f32[5,4,1,128]{3,2,1,0:T(1,128)S(1)}, u32[]{:S(2)}, u32[]{:S(2)}) collective-permute-start(f32[5,4,1,128]{3,2,1,0:T(1,128)S(1)} %get-tuple-element.22), channel_id=1, source_target_pairs={{0,1},{1,2},{2,3},{4,5},{5,6},{6,7},{8,9},{9,10},{10,11},{12,13},{... | collective-permute-start | bytes 30728 | tf_op jit(solution)/shard_map/ppermute | solution.py:19
  101.5 6.8 %collective-permute-start.8 = (f32[4,32,128]{2,1,0:T(8,128)S(1)}, f32[4,32,128]{2,1,0:T(8,128)S(1)}, u32[]{:S(2)}, u32[]{:S(2)}) collective-permute-start(f32[4,32,128]{2,1,0:T(8,128)S(1)} %slice_bitcast_fusion.2), channel_id=1, source_target_pairs={{4,0},{8,4},{12,8},{16,12},{20,16},{24,20},{28,24},{5,1},{9,5},{13... | collective-permute-start | bytes 196616 | tf_op jit(solution)/shard_map/ppermute | solution.py:28
  103.3 5.1 %slice-start = ((f32[4,4,32,128]{3,2,1,0:T(8,128)}), f32[3,4,32,128]{3,2,1,0:T(8,128)S(1)}, s32[]{:S(2)}) async-start(f32[4,4,32,128]{3,2,1,0:T(8,128)} %copy-done), calls=%async_computation.4 | async-start | bytes 393216 | tf_op jit(solution)/shard_map/slice | solution.py:69
  109.8 9.2 %copy-start.1 = (f32[4,4,32,128]{3,2,1,0:T(8,128)S(1)}, f32[4,4,32,128]{3,2,1,0:T(8,128)}, u32[]{:S(2)}) copy-start(f32[4,4,32,128]{3,2,1,0:T(8,128)} %copy-done) | copy-start | bytes 786436
  109.8 9.1 %collective-permute-start.9 = (f32[4,32,128]{2,1,0:T(8,128)S(1)}, f32[4,32,128]{2,1,0:T(8,128)S(1)}, u32[]{:S(2)}, u32[]{:S(2)}) collective-permute-start(f32[4,32,128]{2,1,0:T(8,128)S(1)} %slice_bitcast_fusion), channel_id=1, source_target_pairs={{0,4},{4,8},{8,12},{12,16},{16,20},{20,24},{24,28},{1,5},{5,9},{9,... | collective-permute-start | bytes 196616 | tf_op jit(solution)/shard_map/ppermute | solution.py:28
  114.6 4.4 %collective-permute-start.10 = (f32[4,4,1,128]{3,2,1,0:T(1,128)S(1)}, f32[4,4,1,128]{3,2,1,0:T(1,128)S(1)}, u32[]{:S(2)}, u32[]{:S(2)}) collective-permute-start(f32[4,4,1,128]{3,2,1,0:T(1,128)S(1)} %get-tuple-element.41), channel_id=1, source_target_pairs={{1,0},{2,1},{3,2},{5,4},{6,5},{7,6},{9,8},{10,9},{11,10},{13,12},{... | collective-permute-start | bytes 24584 | tf_op jit(solution)/shard_map/ppermute | solution.py:20
  115.9 3.8 %collective-permute-start.11 = (f32[4,4,1,128]{3,2,1,0:T(1,128)S(1)}, f32[4,4,1,128]{3,2,1,0:T(1,128)S(1)}, u32[]{:S(2)}, u32[]{:S(2)}) collective-permute-start(f32[4,4,1,128]{3,2,1,0:T(1,128)S(1)} %get-tuple-element.42), channel_id=1, source_target_pairs={{0,1},{1,2},{2,3},{4,5},{5,6},{6,7},{8,9},{9,10},{10,11},{12,13},{... | collective-permute-start | bytes 24584 | tf_op jit(solution)/shard_map/ppermute | solution.py:19
